TPU v7x, 32 devices: a whole 2x2x4 slice. The times are simulated.
32 devices in a mesh: slides: 2 (over y), seq: 4 (over z), head: 4 (over x, core).
Axes of the slice: x: 2, y: 2, z: 4, core: 2. Of those that a mesh axis runs over, the one named last changes fastest.
Arguments:
- query_rows: bfloat16 [8192, 768], P(('slides', 'seq'), 'head'), parts along dimension 0, may hold values from -64 to 64
- key_rows: bfloat16 [8192, 768], P(('slides', 'seq'), 'head'), parts along dimension 0, may hold values from -4.1 to 4.1
- value_rows: bfloat16 [8192, 768], P(('slides', 'seq'), 'head'), parts along dimension 0, may hold values from -6 to 6
Outputs:
- attended: bfloat16 [8192, 768], P(('slides', 'seq'), 'head'), parts along dimension 0
There are 2 independent parts, one for each index of `slides`. A program takes and returns all parts, laid end to end along the dimension named above; each array names one. Nothing has to cross between parts.
All inputs are finite; a program needn't handle non-finite values.
Results may differ from a plain program's by a relative error of at most 0.0028.
Values may be sent and summed in bfloat16 or wider, within the bound.
No kernel may reach another device: no remote copies, remote signals or barrier semaphores. Data moves between devices by JAX's collectives and lax.ppermute only.
A program may use at most 64 MiB of HBM per device.

v0:
```python
import math
import jax
import jax.numpy as jnp
import numpy as np
from jax import lax
from jax.sharding import PartitionSpec as P

HEAD_DIM = 48
SEG_A = 1024
SEG_B = 4096


def swapped(shard, axis, stride):
    return lax.ppermute(shard, axis, [(i, i ^ 1 << stride) for i in range(lax.axis_size(axis))])


def attend(query_flat, key_flat, value_flat, score_scale):
    local_heads = query_flat.shape[1] // HEAD_DIM
    query_block = query_flat.reshape(query_flat.shape[0], local_heads, HEAD_DIM)
    key_block = key_flat.reshape(key_flat.shape[0], local_heads, HEAD_DIM)
    value_block = value_flat.reshape(value_flat.shape[0], local_heads, HEAD_DIM)
    scores = (
        jnp.einsum("qad,kad->qak", query_block, key_block, preferred_element_type=jnp.float32)
        * score_scale
    )
    row_max = jnp.max(scores, axis=-1)
    exp_scores = jnp.exp(scores - row_max[:, :, None])
    row_total = jnp.sum(exp_scores, axis=-1)
    weighted = jnp.einsum(
        "qak,kad->qad",
        exp_scores.astype(jnp.bfloat16),
        value_block,
        preferred_element_type=jnp.float32,
    )
    level_out = weighted / row_total[:, :, None]
    return (
        level_out.reshape(query_flat.shape[0], local_heads * HEAD_DIM),
        row_max + jnp.log(row_total),
    )


def attend_rows(query_flat, key_flat, value_flat, score_scale):
    count, feature_width = query_flat.shape
    local_heads = feature_width // HEAD_DIM
    keys = key_flat.shape[0]
    rows = math.gcd(count, max(1, 1048576 // (local_heads * keys)))

    def one_piece(query_piece):
        return attend(query_piece, key_flat, value_flat, score_scale)

    outs, lses = lax.map(one_piece, query_flat.reshape(count // rows, rows, feature_width))
    return (outs.reshape(count, feature_width), lses.reshape(count, local_heads))


def local_segments(query_flat, key_flat, value_flat, seg_rows, score_scale):
    count, feature_width = query_flat.shape
    local_heads = feature_width // HEAD_DIM
    shape = (count // seg_rows, seg_rows, feature_width)

    def one_segment(parts):
        return attend_rows(parts[0], parts[1], parts[2], score_scale)

    outs, lses = lax.map(
        one_segment, (query_flat.reshape(shape), key_flat.reshape(shape), value_flat.reshape(shape))
    )
    return (outs.reshape(count, feature_width), lses.reshape(count, local_heads))


def pick_rows(block, stride):
    row_count, feature_width = block.shape
    local_heads = feature_width // HEAD_DIM
    grid = block.reshape(row_count // stride, stride * feature_width)
    columns = []
    for head in range(local_heads):
        begin = head % stride * feature_width + head * HEAD_DIM
        columns.append(grid[:, begin : begin + HEAD_DIM])
    return jnp.concatenate(columns, axis=1)


def spread_rows(level_out, level_lse, stride):
    used_count, feature_width = level_out.shape
    local_heads = feature_width // HEAD_DIM
    head_of_column = np.arange(feature_width) // HEAD_DIM
    out_phases = []
    lse_phases = []
    for phase in range(stride):
        column_mask = jnp.asarray((head_of_column % stride == phase).astype(np.float32))
        head_mask = jnp.asarray(np.arange(local_heads) % stride == phase)
        out_phases.append(level_out * column_mask[None, :])
        lse_phases.append(jnp.where(head_mask[None, :], level_lse, -jnp.inf))
    full_out = jnp.stack(out_phases, axis=1).reshape(used_count * stride, feature_width)
    full_lse = jnp.stack(lse_phases, axis=1).reshape(used_count * stride, local_heads)
    return (full_out, full_lse)


def fold_block(fold_state, queries, keys, values, valid, score_scale):
    running_max, running_total, running_acc = fold_state
    local_heads = queries.shape[1] // HEAD_DIM
    query_block = queries.reshape(queries.shape[0], local_heads, HEAD_DIM)
    key_block = keys.reshape(keys.shape[0], local_heads, HEAD_DIM)
    value_block = values.reshape(values.shape[0], local_heads, HEAD_DIM)
    scores = (
        jnp.einsum("qad,kad->qak", query_block, key_block, preferred_element_type=jnp.float32)
        * score_scale
    )
    scores = jnp.where(valid[None, None, :], scores, -jnp.inf)
    new_max = jnp.maximum(running_max, jnp.max(scores, axis=-1))
    safe_max = jnp.where(new_max == -jnp.inf, 0.0, new_max)
    rescale = jnp.exp(running_max - safe_max)
    exp_scores = jnp.exp(scores - safe_max[:, :, None])
    new_total = running_total * rescale + jnp.sum(exp_scores, axis=-1)
    weighted = jnp.einsum(
        "qak,kad->qad",
        exp_scores.astype(jnp.bfloat16),
        value_block,
        preferred_element_type=jnp.float32,
    )
    new_acc = running_acc * rescale[:, :, None] + weighted
    return (new_max, new_total, new_acc)


def per_device(query_rows, key_rows, value_rows):
    row_count = query_rows.shape[0]
    feature_width = query_rows.shape[1]
    local_heads = feature_width // HEAD_DIM
    shards = lax.axis_size("seq")
    score_scale = HEAD_DIM ** (-0.5)
    first_out, first_lse = local_segments(query_rows, key_rows, value_rows, SEG_A, score_scale)
    used_two = row_count // 2
    seg_two = SEG_B // 2
    query_two = pick_rows(query_rows, 2)
    key_two = pick_rows(key_rows, 2)
    value_two = pick_rows(value_rows, 2)
    stacked = jnp.stack([key_two, value_two])
    for bit_index in range((seg_two // used_two).bit_length() - 1):
        partner = swapped(stacked, "seq", bit_index)
        stacked = jnp.concatenate([stacked, partner], axis=1)
    second_out, second_lse = attend_rows(query_two, stacked[0], stacked[1], score_scale)
    span_tokens = row_count * shards
    group_span = span_tokens // row_count
    used_three = row_count // 4
    wide_queries = pick_rows(query_rows, 4)
    wide_keys = pick_rows(key_rows, 4)
    wide_values = pick_rows(value_rows, 4)
    my_group = lax.axis_index("seq") // group_span
    key_limit = max(1, 1048576 // (local_heads * used_three))
    initial = (
        jnp.full((used_three, local_heads), -jnp.inf, jnp.float32),
        jnp.zeros((used_three, local_heads), jnp.float32),
        jnp.zeros((used_three, local_heads, HEAD_DIM), jnp.float32),
    )
    pieces = (
        lax.all_gather(wide_keys, "seq", axis=0, tiled=True),
        lax.all_gather(wide_values, "seq", axis=0, tiled=True),
    )
    piece_rows = pieces[0].shape[0]
    block = math.gcd(piece_rows, key_limit)
    key_blocks = pieces[0].reshape(piece_rows // block, block, feature_width)
    value_blocks = pieces[1].reshape(piece_rows // block, block, feature_width)
    block_starts = jnp.arange(piece_rows // block, dtype=jnp.int32) * block

    def fold_step(inner_state, items):
        owners = (items[2] + jnp.arange(block, dtype=jnp.int32)) // used_three
        valid = owners // group_span == my_group
        return (fold_block(inner_state, wide_queries, items[0], items[1], valid, score_scale), None)

    final_state, unused = lax.scan(fold_step, initial, (key_blocks, value_blocks, block_starts))
    final_max, final_total, final_acc = final_state
    third_out = (final_acc / final_total[:, :, None]).reshape(used_three, feature_width)
    third_lse = final_max + jnp.log(final_total)
    second_full, second_lse_full = spread_rows(second_out, second_lse, 2)
    third_full, third_lse_full = spread_rows(third_out, third_lse, 4)
    peak = jnp.maximum(jnp.maximum(first_lse, second_lse_full), third_lse_full)
    weight_one = jnp.exp(first_lse - peak)
    weight_two = jnp.exp(second_lse_full - peak)
    weight_three = jnp.exp(third_lse_full - peak)
    denominator = jnp.repeat(weight_one + weight_two + weight_three, HEAD_DIM, axis=1)
    numerator = jnp.repeat(weight_one, HEAD_DIM, axis=1) * first_out
    numerator = numerator + jnp.repeat(weight_two, HEAD_DIM, axis=1) * second_full
    numerator = numerator + jnp.repeat(weight_three, HEAD_DIM, axis=1) * third_full
    return (numerator / denominator).astype(jnp.bfloat16)


def solution(mesh):
    return jax.shard_map(
        per_device,
        mesh=mesh,
        in_specs=(
            P(("slides", "seq"), "head"),
            P(("slides", "seq"), "head"),
            P(("slides", "seq"), "head"),
        ),
        out_specs=P(("slides", "seq"), "head"),
        check_vma=False,
    )
```

profile of v0, /device:TPU:0, one launch (start us, length us, event | category | flops | bytes accessed | tf_op | source)
XLA Modules:
  0.0 164.0 jit_solution(786289299190109567)
XLA Ops:
  4.0 3.1 %collective-permute-start = (bf16[2,512,192]{2,1,0:T(8,128)(2,1)S(1)}, bf16[2,512,192]{2,1,0:T(8,128)(2,1)S(1)}, u32[]{:S(2)}, u32[]{:S(2)}) collective-permute-start(bf16[2,512,192]{2,1,0:T(8,128)(2,1)S(1)} %pad_maximum_fusion.4), channel_id=1, source_target_pairs={{0,4},{4,0},{8,12},{12,8},{1,5},{5,1},{9,13},{13,9},{2,6},{6,2},{1... | collective-permute-start | bytes 1179656 | tf_op jit(solution)/shard_map/ppermute | solution.py:14
  7.1 1.3 reshape.582
  8.4 1.3 reshape.571
  9.9 1.3 reshape.573
  13.0 19.4 %all_gather.7 = bf16[1024,192]{1,0:T(8,128)(2,1)S(1)} all-gather(bf16[256,192]{1,0:T(8,128)(2,1)S(1)} %pad_maximum_fusion.8), channel_id=1, replica_groups=mesh['slides'=2,'seq'=4,'head'=4] {'seq'}, dimensions={0}, use_global_device_ids=true | all-gather | bytes 491520 | tf_op jit(solution)/shard_map/all_gather | solution.py:154
  33.7 14.8 %all_gather.6 = bf16[1024,192]{1,0:T(8,128)(2,1)S(1)} all-gather(bf16[256,192]{1,0:T(8,128)(2,1)S(1)} %pad_maximum_fusion.6), channel_id=1, replica_groups=mesh['slides'=2,'seq'=4,'head'=4] {'seq'}, dimensions={0}, use_global_device_ids=true | all-gather | bytes 491520 | tf_op jit(solution)/shard_map/all_gather | solution.py:153
  50.1 1.4 bitcast_reduce_fusion.2
  51.5 1.9 %copy-done = f32[4,1024,256]{2,1,0:T(8,128)} copy-done((f32[4,1024,256]{2,1,0:T(8,128)}, f32[4,1024,256]{2,1,0:T(8,128)S(1)}, u32[]{:S(2)}) %copy-start) | copy-done | bytes 4194328
  54.4 35.3 %while.23 = (s32[]{:T(128)}, f32[4,256,192]{1,0,2:T(4,128)}, f32[4,256,4]{1,2,0:T(4,128)}, bf16[4,256,192]{1,2,0:T(8,128)(2,1)S(1)}, bf16[1024,192]{0,1:T(8,128)...) while((s32[]{:T(128)}, f32[4,256,192]{1,0,2:T(4,128)}, f32[4,256,4]{1,2,0:T(4,128)}, ...), condition=%wide.region_3.0_spmd, body=%wide.region_0.3_spmd.sunk | while | flops 209763328 | bytes 16253061 | solution.py:51
  57.4 5.3 %dynamic_update_slice.29 = f32[4,256,192]{1,0,2:T(4,128)} dynamic-update-slice(f32[4,256,192]{1,0,2:T(4,128)} %get-tuple-element.357, f32[1,256,192]{1,0,2:T(1,128)S(1)} %copy.156, s32[]{:T(128)S(6)} %copy.173, s32[]{:T(128)} %constant.135.clone.1..sunk, s32[]{:T(128)} %constant.135.clone.1..sunk) | dynamic-update-slice | bytes 393220 | tf_op jit(solution)/shard_map/while/body/eval_jaxpr/while/body/jit(dynamic_update_index_in_dim)/dynamic_update_slice | solution.py:51
  66.2 5.3 %dynamic_update_slice.29 = f32[4,256,192]{1,0,2:T(4,128)} dynamic-update-slice(f32[4,256,192]{1,0,2:T(4,128)} %get-tuple-element.357, f32[1,256,192]{1,0,2:T(1,128)S(1)} %copy.156, s32[]{:T(128)S(6)} %copy.173, s32[]{:T(128)} %constant.135.clone.1..sunk, s32[]{:T(128)} %constant.135.clone.1..sunk) | dynamic-update-slice | bytes 393220 | tf_op jit(solution)/shard_map/while/body/eval_jaxpr/while/body/jit(dynamic_update_index_in_dim)/dynamic_update_slice | solution.py:51
  75.0 5.3 %dynamic_update_slice.29 = f32[4,256,192]{1,0,2:T(4,128)} dynamic-update-slice(f32[4,256,192]{1,0,2:T(4,128)} %get-tuple-element.357, f32[1,256,192]{1,0,2:T(1,128)S(1)} %copy.156, s32[]{:T(128)S(6)} %copy.173, s32[]{:T(128)} %constant.135.clone.1..sunk, s32[]{:T(128)} %constant.135.clone.1..sunk) | dynamic-update-slice | bytes 393220 | tf_op jit(solution)/shard_map/while/body/eval_jaxpr/while/body/jit(dynamic_update_index_in_dim)/dynamic_update_slice | solution.py:51
  83.9 5.3 %dynamic_update_slice.29 = f32[4,256,192]{1,0,2:T(4,128)} dynamic-update-slice(f32[4,256,192]{1,0,2:T(4,128)} %get-tuple-element.357, f32[1,256,192]{1,0,2:T(1,128)S(1)} %copy.156, s32[]{:T(128)S(6)} %copy.173, s32[]{:T(128)} %constant.135.clone.1..sunk, s32[]{:T(128)} %constant.135.clone.1..sunk) | dynamic-update-slice | bytes 393220 | tf_op jit(solution)/shard_map/while/body/eval_jaxpr/while/body/jit(dynamic_update_index_in_dim)/dynamic_update_slice | solution.py:51
  89.8 3.5 %fusion.38 = f32[256,4,48]{0,2,1:T(8,128)S(1)} fusion(bf16[1024,4,48]{0,2,1:T(8,128)(2,1)} %bitcast.201, f32[4,1024,256]{2,1,0:T(8,128)} %copy-done, f32[256,4]{0,1:T(4,128)S(1)} %compare_select_fusion, pred[1024]{0:T(1024)(128)(4,1)S(1)} %fusion.45, f32[256,4]{0,1:T(4,128)S(1)} %get-tuple-element.237, f32[256,4]{0,1:T(4,128)S(1)} %get-tuple-element.236), kind=kOutput, calls=%fused_computation.35 | convolution fusion | flops 104955904 | bytes 4797440 | tf_op jit(solution)/shard_map/while/body/eval_jaxpr/qak,kad->qad/dot_general | solution.py:112
  99.4 1.3 pad_maximum_fusion.5
  101.5 2.2 %copy.152 = f32[24,8,4,256]{3,1,2,0:T(8,128)} copy(f32[24,8,4,256]{3,2,1,0:T(4,128)} %bitcast.199) | data formatting | bytes 1572864
  104.6 23.1 %collective-permute-done.1 = bf16[2,1024,192]{1,2,0:T(8,128)(2,1)} collective-permute-done((bf16[2,1024,192]{1,2,0:T(8,128)(2,1)}, bf16[2,1024,192]{1,2,0:T(8,128)(2,1)}, u32[]{:S(2)}, u32[]{:S(2)}) %collective-permute-start.1) | collective-permute-done | bytes 786464 | tf_op jit(solution)/shard_map/ppermute | solution.py:14
  127.7 1.3 pad_maximum_fusion
  129.1 29.1 %while.24 = (s32[]{:T(128)}, f32[4,128,192]{1,0,2:T(4,128)}, f32[4,128,4]{1,2,0:T(4,128)S(1)}, bf16[4,128,192]{1,2,0:T(8,128)(2,1)}, bf16[1,2048,192]{1,2,0:T(8,...) while((s32[]{:T(128)}, f32[4,128,192]{1,0,2:T(4,128)}, ...), condition=%wide.region_7.8_spmd, body=%wide.region_4.7_spmd.sunk | while | flops 209739264 | bytes 14614633 | solution.py:51
  132.6 3.9 %dynamic_update_slice.31 = f32[4,128,192]{1,0,2:T(4,128)} dynamic-update-slice(f32[4,128,192]{1,0,2:T(4,128)} %get-tuple-element.333, f32[1,128,192]{1,0,2:T(1,128)S(1)} %bitcast.189, s32[]{:T(128)S(6)} %copy.164, s32[]{:T(128)} %constant.135.clone.1..sunk.1, s32[]{:T(128)} %constant.135.clone.1..sunk.1) | dynamic-update-slice | bytes 196612 | tf_op jit(solution)/shard_map/while/body/jit(dynamic_update_index_in_dim)/dynamic_update_slice | solution.py:51
  139.8 3.9 %dynamic_update_slice.31 = f32[4,128,192]{1,0,2:T(4,128)} dynamic-update-slice(f32[4,128,192]{1,0,2:T(4,128)} %get-tuple-element.333, f32[1,128,192]{1,0,2:T(1,128)S(1)} %bitcast.189, s32[]{:T(128)S(6)} %copy.164, s32[]{:T(128)} %constant.135.clone.1..sunk.1, s32[]{:T(128)} %constant.135.clone.1..sunk.1) | dynamic-update-slice | bytes 196612 | tf_op jit(solution)/shard_map/while/body/jit(dynamic_update_index_in_dim)/dynamic_update_slice | solution.py:51
  147.1 3.9 %dynamic_update_slice.31 = f32[4,128,192]{1,0,2:T(4,128)} dynamic-update-slice(f32[4,128,192]{1,0,2:T(4,128)} %get-tuple-element.333, f32[1,128,192]{1,0,2:T(1,128)S(1)} %bitcast.189, s32[]{:T(128)S(6)} %copy.164, s32[]{:T(128)} %constant.135.clone.1..sunk.1, s32[]{:T(128)} %constant.135.clone.1..sunk.1) | dynamic-update-slice | bytes 196612 | tf_op jit(solution)/shard_map/while/body/jit(dynamic_update_index_in_dim)/dynamic_update_slice | solution.py:51
  154.4 3.9 %dynamic_update_slice.31 = f32[4,128,192]{1,0,2:T(4,128)} dynamic-update-slice(f32[4,128,192]{1,0,2:T(4,128)} %get-tuple-element.333, f32[1,128,192]{1,0,2:T(1,128)S(1)} %bitcast.189, s32[]{:T(128)S(6)} %copy.164, s32[]{:T(128)} %constant.135.clone.1..sunk.1, s32[]{:T(128)} %constant.135.clone.1..sunk.1) | dynamic-update-slice | bytes 196612 | tf_op jit(solution)/shard_map/while/body/jit(dynamic_update_index_in_dim)/dynamic_update_slice | solution.py:51
  161.9 2.2 %fusion.41 = bf16[1024,192]{0,1:T(8,128)(2,1)} fusion(f32[1024,192]{0,1:T(8,128)S(1)} %copy.142, f32[1024,192]{0,1:T(8,128)S(1)} %copy.137, f32[1024,192]{0,1:T(8,128)} %bitcast.193, f32[1024,4]{0,1:T(4,128)S(1)} %get-tuple-element.189, f32[1024,4]{0,1:T(4,128)S(1)} %get-tuple-element.192, f32[1024,4]{0,1:T(4,128)S(1)} %get-tuple-element.190, ...), kind=kLoop, calls=%fused_computation.40 | loop fusion | flops 1376256 | bytes 2818048 | tf_op jit(solution)/shard_map/convert_element_type | solution.py:181
  (145 shorter events, 49.0 us)
Async XLA Ops:
  2.4 7.2 %copy-start.2 = (bf16[1024,192]{0,1:T(8,128)(2,1)S(1)}, bf16[1024,192]{0,1:T(8,128)(2,1)}, u32[]{:S(2)}) copy-start(bf16[1024,192]{0,1:T(8,128)(2,1)} %param.19) | copy-start | bytes 1179652
  4.0 91.0 %collective-permute-start = (bf16[2,512,192]{2,1,0:T(8,128)(2,1)S(1)}, bf16[2,512,192]{2,1,0:T(8,128)(2,1)S(1)}, u32[]{:S(2)}, u32[]{:S(2)}) collective-permute-start(bf16[2,512,192]{2,1,0:T(8,128)(2,1)S(1)} %pad_maximum_fusion.4), channel_id=1, source_target_pairs={{0,4},{4,0},{8,12},{12,8},{1,5},{5,1},{9,13},{13,9},{2,6},{6,2},{1... | collective-permute-start | bytes 1179656 | tf_op jit(solution)/shard_map/ppermute | solution.py:14
  9.9 23.6 %copy-start.4 = (bf16[256,768]{1,0:T(8,128)(2,1)S(1)}, bf16[256,768]{1,0:T(8,128)(2,1)}, u32[]{:S(2)}) copy-start(bf16[256,768]{1,0:T(8,128)(2,1)} %reshape.571) | copy-start | bytes 1179652
  50.1 4.3 %copy-start.3 = (bf16[1024,192]{0,1:T(8,128)(2,1)S(1)}, bf16[1024,192]{0,1:T(8,128)(2,1)}, u32[]{:S(2)}) copy-start(bf16[1024,192]{0,1:T(8,128)(2,1)} %param.19) | copy-start | bytes 1179652
  50.1 4.3 %copy-start.1 = (bf16[1024,192]{0,1:T(8,128)(2,1)S(1)}, bf16[1024,192]{0,1:T(8,128)(2,1)}, u32[]{:S(2)}) copy-start(bf16[1024,192]{0,1:T(8,128)(2,1)} %param.20) | copy-start | bytes 1179652
  51.5 1.9 %copy-start = (f32[4,1024,256]{2,1,0:T(8,128)}, f32[4,1024,256]{2,1,0:T(8,128)S(1)}, u32[]{:S(2)}) copy-start(f32[4,1024,256]{2,1,0:T(8,128)S(1)} %get-tuple-element.239) | copy-start | bytes 12582916
  54.5 1.8 %copy-start.5 = (bf16[1024,192]{0,1:T(8,128)(2,1)S(1)}, bf16[1024,192]{0,1:T(8,128)(2,1)}, u32[]{:S(2)}) copy-start(bf16[1024,192]{0,1:T(8,128)(2,1)} %get-tuple-element.369) | copy-start | bytes 1179652 | tf_op jit(solution)/shard_map/while/body/eval_jaxpr/while
  63.3 1.8 %copy-start.5 = (bf16[1024,192]{0,1:T(8,128)(2,1)S(1)}, bf16[1024,192]{0,1:T(8,128)(2,1)}, u32[]{:S(2)}) copy-start(bf16[1024,192]{0,1:T(8,128)(2,1)} %get-tuple-element.369) | copy-start | bytes 1179652 | tf_op jit(solution)/shard_map/while/body/eval_jaxpr/while
  72.1 1.8 %copy-start.5 = (bf16[1024,192]{0,1:T(8,128)(2,1)S(1)}, bf16[1024,192]{0,1:T(8,128)(2,1)}, u32[]{:S(2)}) copy-start(bf16[1024,192]{0,1:T(8,128)(2,1)} %get-tuple-element.369) | copy-start | bytes 1179652 | tf_op jit(solution)/shard_map/while/body/eval_jaxpr/while
  80.9 1.8 %copy-start.5 = (bf16[1024,192]{0,1:T(8,128)(2,1)S(1)}, bf16[1024,192]{0,1:T(8,128)(2,1)}, u32[]{:S(2)}) copy-start(bf16[1024,192]{0,1:T(8,128)(2,1)} %get-tuple-element.369) | copy-start | bytes 1179652 | tf_op jit(solution)/shard_map/while/body/eval_jaxpr/while
  89.7 4.4 %copy-start.9 = (f32[192]{0:T(256)S(1)}, f32[192]{0:T(256)}, u32[]{:S(2)}) copy-start(f32[192]{0:T(256)} %constant.151.clone) | copy-start | bytes 2308
  89.7 4.4 %copy-start.10 = (f32[192]{0:T(256)S(1)}, f32[192]{0:T(256)}, u32[]{:S(2)}) copy-start(f32[192]{0:T(256)} %constant.153.clone) | copy-start | bytes 2308
  89.8 4.4 %copy-start.11 = (f32[192]{0:T(256)S(1)}, f32[192]{0:T(256)}, u32[]{:S(2)}) copy-start(f32[192]{0:T(256)} %constant.155.clone) | copy-start | bytes 2308
  89.8 4.4 %copy-start.12 = (f32[192]{0:T(256)S(1)}, f32[192]{0:T(256)}, u32[]{:S(2)}) copy-start(f32[192]{0:T(256)} %constant.157.clone) | copy-start | bytes 2308
  96.5 31.2 %collective-permute-start.1 = (bf16[2,1024,192]{1,2,0:T(8,128)(2,1)}, bf16[2,1024,192]{1,2,0:T(8,128)(2,1)}, u32[]{:S(2)}, u32[]{:S(2)}) collective-permute-start(bf16[2,1024,192]{1,2,0:T(8,128)(2,1)} %copy.122), channel_id=1, source_target_pairs={{0,8},{4,12},{8,0},{12,4},{1,9},{5,13},{9,1},{13,5},{2,10},{6,14},... | collective-permute-start | bytes 2359304 | tf_op jit(solution)/shard_map/ppermute | solution.py:14
  98.3 5.4 %copy-start.18 = (pred[4]{0:T(512)(128)(4,1)S(1)}, pred[4]{0:T(512)(128)(4,1)}, u32[]{:S(2)}) copy-start(pred[4]{0:T(512)(128)(4,1)} %constant.152.clone) | copy-start | bytes 16
  98.3 5.5 %copy-start.15 = (pred[4]{0:T(512)(128)(4,1)S(1)}, pred[4]{0:T(512)(128)(4,1)}, u32[]{:S(2)}) copy-start(pred[4]{0:T(512)(128)(4,1)} %constant.154.clone) | copy-start | bytes 16
  98.3 5.5 %copy-start.16 = (pred[4]{0:T(512)(128)(4,1)S(1)}, pred[4]{0:T(512)(128)(4,1)}, u32[]{:S(2)}) copy-start(pred[4]{0:T(512)(128)(4,1)} %constant.156.clone) | copy-start | bytes 16
  98.3 5.5 %copy-start.17 = (pred[4]{0:T(512)(128)(4,1)S(1)}, pred[4]{0:T(512)(128)(4,1)}, u32[]{:S(2)}) copy-start(pred[4]{0:T(512)(128)(4,1)} %constant.158.clone) | copy-start | bytes 16
  129.1 30.3 %copy-start.7 = (f32[192]{0:T(256)S(1)}, f32[192]{0:T(256)}, u32[]{:S(2)}) copy-start(f32[192]{0:T(256)} %constant.147.clone) | copy-start | bytes 2308
  129.1 30.3 %copy-start.8 = (f32[192]{0:T(256)S(1)}, f32[192]{0:T(256)}, u32[]{:S(2)}) copy-start(f32[192]{0:T(256)} %constant.149.clone) | copy-start | bytes 2308
  159.4 1.8 %copy-start.13 = (pred[4]{0:T(512)(128)(4,1)S(1)}, pred[4]{0:T(512)(128)(4,1)}, u32[]{:S(2)}) copy-start(pred[4]{0:T(512)(128)(4,1)} %constant.148.clone) | copy-start | bytes 16
  159.4 1.8 %copy-start.14 = (pred[4]{0:T(512)(128)(4,1)S(1)}, pred[4]{0:T(512)(128)(4,1)}, u32[]{:S(2)}) copy-start(pred[4]{0:T(512)(128)(4,1)} %constant.150.clone) | copy-start | bytes 16
  159.6 2.3 %copy-start.6 = (f32[4,256,4]{1,2,0:T(4,128)S(1)}, f32[4,256,4]{1,2,0:T(4,128)}, u32[]{:S(2)}) copy-start(f32[4,256,4]{1,2,0:T(4,128)} %get-tuple-element.113) | copy-start | bytes 49156
where the time goes:
time: 165 us; the launch traced here: 164 us
  local copies, waits for them, and re-layouts  64.5 us (39%)
  blocking collectives  34.2 us (21%)
  waiting for transfers between devices  23.1 us (14%)
  matrix products  18.9 us (11%)
  other arithmetic  18.8 us (11%)
  starting transfers between devices  3.83 us (2%)
    dynamic_update_slice x12, local copies, waits for them, and re-layouts, attend_rows(): lax.map(one_piece, query_flat.reshape(count // rows, rows, feature_width))  37.4 us
    ppermute x2, waiting for transfers between devices, swapped(): lax.ppermute(shard, axis, [(i, i ^ 1 << stride) for i in range(lax.axis_s...  23.1 us
    all_gather x1, blocking collectives, per_device(): lax.all_gather(wide_values, 'seq', axis=0, tiled=True)  19.4 us
    all_gather x1, blocking collectives, per_device(): lax.all_gather(wide_keys, 'seq', axis=0, tiled=True)  14.8 us
    dot_general x8, matrix products, attend(): jnp.einsum('qak,kad->qad', exp_scores.astype(jnp.bfloat16), value_block,...  7.47 us
    reduce_sum x8, other arithmetic, attend(): row_total = jnp.sum(exp_scores, axis=-1)  7.01 us
    unnamed x40, local copies, waits for them, and re-layouts  6.78 us
    dot_general x8, matrix products, attend(): jnp.einsum('qad,kad->qak', query_block, key_block, preferred_element_type...  6.63 us
  transfers between devices with their start and end apart: 2, of which 1 were waited for; matrix products, arithmetic and copies ran while one was open for 36% of the time, Pallas kernels for 0%

commit v1 on v0

--- a/solution.py
+++ b/solution.py
@@ -8,6 +8,27 @@
 HEAD_DIM = 48
 SEG_A = 1024
 SEG_B = 4096
+
+
+def ring_gather(array, axis, dim):
+    length, index, width = (lax.axis_size(axis), lax.axis_index(axis), array.shape[dim])
+    ahead = [(i, (i + 1) % length) for i in range(length)]
+    backward = [(i, (i - 1) % length) for i in range(length)]
+    result = jnp.zeros((*array.shape[:dim], length * width, *array.shape[dim + 1 :]), array.dtype)
+    result = lax.dynamic_update_slice_in_dim(result, array, index * width, axis=dim)
+    from_left = from_right = array
+    half = length // 2
+    for turn in range(1, half + 1):
+        from_left = lax.ppermute(from_left, axis, ahead)
+        result = lax.dynamic_update_slice_in_dim(
+            result, from_left, (index - turn) % length * width, axis=dim
+        )
+        if turn < length - half:
+            from_right = lax.ppermute(from_right, axis, backward)
+            result = lax.dynamic_update_slice_in_dim(
+                result, from_right, (index + turn) % length * width, axis=dim
+            )
+    return result
 
 
 def swapped(shard, axis, stride):
@@ -151,7 +172,7 @@
     )
     pieces = (
         lax.all_gather(wide_keys, "seq", axis=0, tiled=True),
-        lax.all_gather(wide_values, "seq", axis=0, tiled=True),
+        ring_gather(wide_values, "seq", 0),
     )
     piece_rows = pieces[0].shape[0]
     block = math.gcd(piece_rows, key_limit)

time: 165 us -> 158 us (0.958)
  blocking collectives: 34.2 us -> 22.7 us
  waiting for transfers between devices: 23.1 us -> 32.2 us
  local copies, waits for them, and re-layouts: 64.5 us -> 60.2 us
  other arithmetic: 18.8 us -> 16 us
  starting transfers between devices: 3.83 us -> 5.73 us
    all_gather x1 -> x0, blocking collectives: 19.4 us -> none  [per_device(): lax.all_gather(wide_values, 'seq', axis=0, tiled=True)]
    all_gather x1, blocking collectives: 14.8 us -> 22.7 us  [per_device(): lax.all_gather(wide_keys, 'seq', axis=0, tiled=True)]
    ppermute x0 -> x3, waiting for transfers between devices: none -> 6.48 us  [the longest x2 6.48 us: ring_gather(): from_left = lax.ppermute(from_left, axis, ahead)]
    ppermute x0 -> x3, starting transfers between devices: none -> 5.66 us  [the longest x2 3.56 us: ring_gather(): from_left = lax.ppermute(from_left, axis, ahead)]
    ppermute x2, starting transfers between devices: 3.83 us -> 0.07 us  [swapped(): lax.ppermute(shard, axis, [(i, i ^ 1 << stride) for i in range(lax.axis_s...]
    dynamic_slice x8, local copies, waits for them, and re-layouts: 3.26 us -> 0.06 us  [attend_rows(): lax.map(one_piece, query_flat.reshape(count // rows, rows, feature_width))]
    ppermute x2, waiting for transfers between devices: 23.1 us -> 25.8 us  [swapped(): lax.ppermute(shard, axis, [(i, i ^ 1 << stride) for i in range(lax.axis_s...]
    ppermute x0 -> x3, local copies, waits for them, and re-layouts: none -> 2.1 us  [the longest x2 1.1 us: ring_gather(): from_left = lax.ppermute(from_left, axis, ahead)]
  transfers between devices with their start and end apart: 2 -> 5, of which waited for: 1 -> 2; matrix products, arithmetic and copies ran while one was open for 36% -> 36% of each run, Pallas kernels for 0% -> 0%
where the time goes in v1:
time: 158 us; the launch traced here: 157 us
  local copies, waits for them, and re-layouts  60.2 us (38%)
  waiting for transfers between devices  32.2 us (20%)
  blocking collectives  22.7 us (14%)
  matrix products  18.7 us (12%)
  other arithmetic  16 us (10%)
  starting transfers between devices  5.73 us (4%)
    dynamic_update_slice x12, local copies, waits for them, and re-layouts, attend_rows(): lax.map(one_piece, query_flat.reshape(count // rows, rows, feature_width))  37.6 us
    ppermute x2, waiting for transfers between devices, swapped(): lax.ppermute(shard, axis, [(i, i ^ 1 << stride) for i in range(lax.axis_s...  25.8 us
    all_gather x1, blocking collectives, per_device(): lax.all_gather(wide_keys, 'seq', axis=0, tiled=True)  22.7 us
    dot_general x8, matrix products, attend(): jnp.einsum('qak,kad->qad', exp_scores.astype(jnp.bfloat16), value_block,...  7.47 us
    reduce_sum x8, other arithmetic, attend(): row_total = jnp.sum(exp_scores, axis=-1)  7.01 us
    unnamed x40, local copies, waits for them, and re-layouts  6.78 us
    dot_general x8, matrix products, attend(): jnp.einsum('qad,kad->qak', query_block, key_block, preferred_element_type...  6.65 us
    ppermute x2, waiting for transfers between devices, ring_gather(): from_left = lax.ppermute(from_left, axis, ahead)  6.48 us
  transfers between devices with their start and end apart: 5, of which 2 were waited for; matrix products, arithmetic and copies ran while one was open for 36% of the time, Pallas kernels for 0%

profile of v1, /device:TPU:0, one launch (start us, length us, event | category | flops | bytes accessed | tf_op | source)
XLA Modules:
  0.0 156.6 jit_solution(12595411561614695174)
XLA Ops:
  2.0 3.1 %collective-permute-start.2 = (bf16[256,192]{1,0:T(8,128)(2,1)S(1)}, bf16[256,192]{1,0:T(8,128)(2,1)}, u32[]{:S(2)}, u32[]{:S(2)}) collective-permute-start(bf16[256,192]{1,0:T(8,128)(2,1)S(1)} %pad_maximum_fusion.8), channel_id=1, source_target_pairs={{0,4},{4,8},{8,12},{12,0},{1,5},{5,9},{9,13},{13,1},{2,6},{6,10},{... | collective-permute-start | bytes 294920 | tf_op jit(solution)/shard_map/ppermute | solution.py:22
  5.1 2.1 %collective-permute-start.3 = (bf16[256,192]{1,0:T(8,128)(2,1)S(1)}, bf16[256,192]{1,0:T(8,128)(2,1)}, u32[]{:S(2)}, u32[]{:S(2)}) collective-permute-start(bf16[256,192]{1,0:T(8,128)(2,1)S(1)} %pad_maximum_fusion.8), channel_id=1, source_target_pairs={{0,12},{4,0},{8,4},{12,8},{1,13},{5,1},{9,5},{13,9},{2,14},{6,2},{... | collective-permute-start | bytes 294920 | tf_op jit(solution)/shard_map/ppermute | solution.py:27
  7.5 1.2 copy.129
  10.8 1.3 reshape.590
  12.8 22.7 %all_gather.3 = bf16[1024,192]{1,0:T(8,128)(2,1)S(1)} all-gather(bf16[256,192]{1,0:T(8,128)(2,1)S(1)} %pad_maximum_fusion.6), channel_id=1, replica_groups=mesh['slides'=2,'seq'=4,'head'=4] {'seq'}, dimensions={0}, use_global_device_ids=true | all-gather | bytes 491520 | tf_op jit(solution)/shard_map/all_gather | solution.py:174
  37.1 1.2 bitcast_reduce_fusion.2
  38.4 1.9 %copy-done = f32[4,1024,256]{2,1,0:T(8,128)} copy-done((f32[4,1024,256]{2,1,0:T(8,128)}, f32[4,1024,256]{2,1,0:T(8,128)S(1)}, u32[]{:S(2)}) %copy-start) | copy-done | bytes 4194328
  42.2 35.5 %while.23 = (s32[]{:T(128)}, f32[4,256,192]{1,0,2:T(4,128)}, f32[4,256,4]{1,2,0:T(4,128)}, bf16[4,256,192]{1,2,0:T(8,128)(2,1)S(1)}, bf16[1024,192]{0,1:T(8,128)...) while((s32[]{:T(128)}, f32[4,256,192]{1,0,2:T(4,128)}, f32[4,256,4]{1,2,0:T(4,128)}, ...), condition=%wide.region_3.0_spmd, body=%wide.region_0.3_spmd.sunk | while | flops 209763328 | bytes 16253061 | solution.py:72
  45.1 5.3 %dynamic_update_slice.57 = f32[4,256,192]{1,0,2:T(4,128)} dynamic-update-slice(f32[4,256,192]{1,0,2:T(4,128)} %get-tuple-element.357, f32[1,256,192]{1,0,2:T(1,128)S(1)} %copy.168, s32[]{:T(128)S(6)} %copy.189, s32[]{:T(128)} %constant.167.clone.1..sunk, s32[]{:T(128)} %constant.167.clone.1..sunk) | dynamic-update-slice | bytes 393220 | tf_op jit(solution)/shard_map/while/body/eval_jaxpr/while/body/jit(dynamic_update_index_in_dim)/dynamic_update_slice | solution.py:72
  54.0 5.3 %dynamic_update_slice.57 = f32[4,256,192]{1,0,2:T(4,128)} dynamic-update-slice(f32[4,256,192]{1,0,2:T(4,128)} %get-tuple-element.357, f32[1,256,192]{1,0,2:T(1,128)S(1)} %copy.168, s32[]{:T(128)S(6)} %copy.189, s32[]{:T(128)} %constant.167.clone.1..sunk, s32[]{:T(128)} %constant.167.clone.1..sunk) | dynamic-update-slice | bytes 393220 | tf_op jit(solution)/shard_map/while/body/eval_jaxpr/while/body/jit(dynamic_update_index_in_dim)/dynamic_update_slice | solution.py:72
  62.8 5.3 %dynamic_update_slice.57 = f32[4,256,192]{1,0,2:T(4,128)} dynamic-update-slice(f32[4,256,192]{1,0,2:T(4,128)} %get-tuple-element.357, f32[1,256,192]{1,0,2:T(1,128)S(1)} %copy.168, s32[]{:T(128)S(6)} %copy.189, s32[]{:T(128)} %constant.167.clone.1..sunk, s32[]{:T(128)} %constant.167.clone.1..sunk) | dynamic-update-slice | bytes 393220 | tf_op jit(solution)/shard_map/while/body/eval_jaxpr/while/body/jit(dynamic_update_index_in_dim)/dynamic_update_slice | solution.py:72
  71.7 5.3 %dynamic_update_slice.57 = f32[4,256,192]{1,0,2:T(4,128)} dynamic-update-slice(f32[4,256,192]{1,0,2:T(4,128)} %get-tuple-element.357, f32[1,256,192]{1,0,2:T(1,128)S(1)} %copy.168, s32[]{:T(128)S(6)} %copy.189, s32[]{:T(128)} %constant.167.clone.1..sunk, s32[]{:T(128)} %constant.167.clone.1..sunk) | dynamic-update-slice | bytes 393220 | tf_op jit(solution)/shard_map/while/body/eval_jaxpr/while/body/jit(dynamic_update_index_in_dim)/dynamic_update_slice | solution.py:72
  78.6 2.2 %copy.164 = f32[24,8,4,256]{3,1,2,0:T(8,128)} copy(f32[24,8,4,256]{3,2,1,0:T(4,128)} %bitcast.38) | data formatting | bytes 1572864
  84.0 6.5 %collective-permute-done.4 = bf16[256,192]{1,0:T(8,128)(2,1)S(1)} collective-permute-done((bf16[256,192]{1,0:T(8,128)(2,1)}, bf16[256,192]{1,0:T(8,128)(2,1)S(1)}, u32[]{:S(2)}, u32[]{:S(2)}) %collective-permute-start.4) | collective-permute-done | bytes 98336 | tf_op jit(solution)/shard_map/ppermute | solution.py:22
  90.8 1.2 copy.131
  92.7 3.4 %fusion.38 = f32[256,4,48]{0,2,1:T(8,128)S(1)} fusion(bf16[1024,4,48]{0,2,1:T(8,128)(2,1)} %bitcast.200, f32[4,1024,256]{2,1,0:T(8,128)} %copy-done, f32[256,4]{0,1:T(4,128)S(1)} %compare_select_fusion, pred[1024]{0:T(1024)(128)(4,1)S(1)} %fusion.45, f32[256,4]{0,1:T(4,128)S(1)} %get-tuple-element.237, f32[256,4]{0,1:T(4,128)S(1)} %get-tuple-element.236), kind=kOutput, calls=%fused_computation.35 | convolution fusion | flops 104955904 | bytes 4797440 | tf_op jit(solution)/shard_map/while/body/eval_jaxpr/qak,kad->qad/dot_general | solution.py:133
  97.7 25.8 %collective-permute-done.1 = bf16[2,1024,192]{1,2,0:T(8,128)(2,1)} collective-permute-done((bf16[2,1024,192]{1,2,0:T(8,128)(2,1)}, bf16[2,1024,192]{1,2,0:T(8,128)(2,1)}, u32[]{:S(2)}, u32[]{:S(2)}) %collective-permute-start.1) | collective-permute-done | bytes 786464 | tf_op jit(solution)/shard_map/ppermute | solution.py:35
  123.4 1.3 pad_maximum_fusion
  124.9 26.0 %while.24 = (s32[]{:T(128)}, f32[4,128,192]{1,0,2:T(4,128)}, f32[4,128,4]{1,2,0:T(4,128)S(1)}, bf16[4,128,192]{1,2,0:T(8,128)(2,1)S(1)}, bf16[1,2048,192]{1,2,0:...) while((s32[]{:T(128)}, f32[4,128,192]{1,0,2:T(4,128)}, ...), condition=%wide.region_7.8_spmd, body=%wide.region_4.7_spmd.sunk | while | flops 209739264 | bytes 14614633 | solution.py:72
  127.5 3.9 %dynamic_update_slice.59 = f32[4,128,192]{1,0,2:T(4,128)} dynamic-update-slice(f32[4,128,192]{1,0,2:T(4,128)} %get-tuple-element.333, f32[1,128,192]{1,0,2:T(1,128)S(1)} %bitcast.189, s32[]{:T(128)S(6)} %copy.180, s32[]{:T(128)} %constant.167.clone.1..sunk.1, s32[]{:T(128)} %constant.167.clone.1..sunk.1) | dynamic-update-slice | bytes 196612 | tf_op jit(solution)/shard_map/while/body/jit(dynamic_update_index_in_dim)/dynamic_update_slice | solution.py:72
  134.0 3.9 %dynamic_update_slice.59 = f32[4,128,192]{1,0,2:T(4,128)} dynamic-update-slice(f32[4,128,192]{1,0,2:T(4,128)} %get-tuple-element.333, f32[1,128,192]{1,0,2:T(1,128)S(1)} %bitcast.189, s32[]{:T(128)S(6)} %copy.180, s32[]{:T(128)} %constant.167.clone.1..sunk.1, s32[]{:T(128)} %constant.167.clone.1..sunk.1) | dynamic-update-slice | bytes 196612 | tf_op jit(solution)/shard_map/while/body/jit(dynamic_update_index_in_dim)/dynamic_update_slice | solution.py:72
  140.5 3.9 %dynamic_update_slice.59 = f32[4,128,192]{1,0,2:T(4,128)} dynamic-update-slice(f32[4,128,192]{1,0,2:T(4,128)} %get-tuple-element.333, f32[1,128,192]{1,0,2:T(1,128)S(1)} %bitcast.189, s32[]{:T(128)S(6)} %copy.180, s32[]{:T(128)} %constant.167.clone.1..sunk.1, s32[]{:T(128)} %constant.167.clone.1..sunk.1) | dynamic-update-slice | bytes 196612 | tf_op jit(solution)/shard_map/while/body/jit(dynamic_update_index_in_dim)/dynamic_update_slice | solution.py:72
  147.0 3.9 %dynamic_update_slice.59 = f32[4,128,192]{1,0,2:T(4,128)} dynamic-update-slice(f32[4,128,192]{1,0,2:T(4,128)} %get-tuple-element.333, f32[1,128,192]{1,0,2:T(1,128)S(1)} %bitcast.189, s32[]{:T(128)S(6)} %copy.180, s32[]{:T(128)} %constant.167.clone.1..sunk.1, s32[]{:T(128)} %constant.167.clone.1..sunk.1) | dynamic-update-slice | bytes 196612 | tf_op jit(solution)/shard_map/while/body/jit(dynamic_update_index_in_dim)/dynamic_update_slice | solution.py:72
  154.5 2.2 %fusion.41 = bf16[1024,192]{0,1:T(8,128)(2,1)} fusion(f32[1024,192]{0,1:T(8,128)S(1)} %copy.154, f32[1024,192]{0,1:T(8,128)S(1)} %copy.146, f32[1024,192]{0,1:T(8,128)} %bitcast.193, f32[1024,4]{0,1:T(4,128)S(1)} %get-tuple-element.189, f32[1024,4]{0,1:T(4,128)S(1)} %get-tuple-element.192, f32[1024,4]{0,1:T(4,128)S(1)} %get-tuple-element.190, ...), kind=kLoop, calls=%fused_computation.40 | loop fusion | flops 1376256 | bytes 2818048 | tf_op jit(solution)/shard_map/convert_element_type | solution.py:202
  (158 shorter events, 42.9 us)
Async XLA Ops:
  2.0 8.6 %copy-start.2 = (bf16[1024,192]{0,1:T(8,128)(2,1)S(1)}, bf16[1024,192]{0,1:T(8,128)(2,1)}, u32[]{:S(2)}) copy-start(bf16[1024,192]{0,1:T(8,128)(2,1)} %param.19) | copy-start | bytes 1179652
  2.0 79.4 %collective-permute-start.2 = (bf16[256,192]{1,0:T(8,128)(2,1)S(1)}, bf16[256,192]{1,0:T(8,128)(2,1)}, u32[]{:S(2)}, u32[]{:S(2)}) collective-permute-start(bf16[256,192]{1,0:T(8,128)(2,1)S(1)} %pad_maximum_fusion.8), channel_id=1, source_target_pairs={{0,4},{4,8},{8,12},{12,0},{1,5},{5,9},{9,13},{13,1},{2,6},{6,10},{... | collective-permute-start | bytes 294920 | tf_op jit(solution)/shard_map/ppermute | solution.py:22
  5.1 77.8 %collective-permute-start.3 = (bf16[256,192]{1,0:T(8,128)(2,1)S(1)}, bf16[256,192]{1,0:T(8,128)(2,1)}, u32[]{:S(2)}, u32[]{:S(2)}) collective-permute-start(bf16[256,192]{1,0:T(8,128)(2,1)S(1)} %pad_maximum_fusion.8), channel_id=1, source_target_pairs={{0,12},{4,0},{8,4},{12,8},{1,13},{5,1},{9,5},{13,9},{2,14},{6,2},{... | collective-permute-start | bytes 294920 | tf_op jit(solution)/shard_map/ppermute | solution.py:27
  10.0 80.5 %collective-permute-start = (bf16[2,512,192]{2,1,0:T(8,128)(2,1)S(1)}, bf16[2,512,192]{2,1,0:T(8,128)(2,1)S(1)}, u32[]{:S(2)}, u32[]{:S(2)}) collective-permute-start(bf16[2,512,192]{2,1,0:T(8,128)(2,1)S(1)} %pad_maximum_fusion.4), channel_id=1, source_target_pairs={{0,4},{4,0},{8,12},{12,8},{1,5},{5,1},{9,13},{13,9},{2,6},{6,2},{1... | collective-permute-start | bytes 1179656 | tf_op jit(solution)/shard_map/ppermute | solution.py:35
  38.4 1.9 %copy-start = (f32[4,1024,256]{2,1,0:T(8,128)}, f32[4,1024,256]{2,1,0:T(8,128)S(1)}, u32[]{:S(2)}) copy-start(f32[4,1024,256]{2,1,0:T(8,128)S(1)} %get-tuple-element.239) | copy-start | bytes 12582916
  38.4 3.7 %copy-start.1 = (bf16[1024,192]{0,1:T(8,128)(2,1)S(1)}, bf16[1024,192]{0,1:T(8,128)(2,1)}, u32[]{:S(2)}) copy-start(bf16[1024,192]{0,1:T(8,128)(2,1)} %param.20) | copy-start | bytes 1179652
  42.1 35.5 %copy-start.18 = (pred[4]{0:T(512)(128)(4,1)S(1)}, pred[4]{0:T(512)(128)(4,1)}, u32[]{:S(2)}) copy-start(pred[4]{0:T(512)(128)(4,1)} %constant.189.clone) | copy-start | bytes 16
  42.1 35.6 %copy-start.3 = (bf16[512,48]{1,0:T(8,128)(2,1)S(1)}, bf16[512,48]{1,0:T(8,128)(2,1)}, u32[]{:S(2)}) copy-start(bf16[512,48]{1,0:T(8,128)(2,1)} %get-tuple-element.214) | copy-start | bytes 147460
  42.1 35.8 %copy-start.15 = (pred[4]{0:T(512)(128)(4,1)S(1)}, pred[4]{0:T(512)(128)(4,1)}, u32[]{:S(2)}) copy-start(pred[4]{0:T(512)(128)(4,1)} %constant.191.clone) | copy-start | bytes 16
  42.1 35.8 %copy-start.16 = (pred[4]{0:T(512)(128)(4,1)S(1)}, pred[4]{0:T(512)(128)(4,1)}, u32[]{:S(2)}) copy-start(pred[4]{0:T(512)(128)(4,1)} %constant.193.clone) | copy-start | bytes 16
  42.1 35.8 %copy-start.17 = (pred[4]{0:T(512)(128)(4,1)S(1)}, pred[4]{0:T(512)(128)(4,1)}, u32[]{:S(2)}) copy-start(pred[4]{0:T(512)(128)(4,1)} %constant.195.clone) | copy-start | bytes 16
  42.2 1.8 %copy-start.4 = (bf16[1024,192]{0,1:T(8,128)(2,1)S(1)}, bf16[1024,192]{0,1:T(8,128)(2,1)}, u32[]{:S(2)}) copy-start(bf16[1024,192]{0,1:T(8,128)(2,1)} %get-tuple-element.369) | copy-start | bytes 1179652 | tf_op jit(solution)/shard_map/while/body/eval_jaxpr/while
  82.4 8.0 %collective-permute-start.4 = (bf16[256,192]{1,0:T(8,128)(2,1)}, bf16[256,192]{1,0:T(8,128)(2,1)S(1)}, u32[]{:S(2)}, u32[]{:S(2)}) collective-permute-start(bf16[256,192]{1,0:T(8,128)(2,1)} %collective-permute-done.2), channel_id=1, source_target_pairs={{0,4},{4,8},{8,12},{12,0},{1,5},{5,9},{9,13},{13,1},{2,6},{6,10},{... | collective-permute-start | bytes 294920 | tf_op jit(solution)/shard_map/ppermute | solution.py:22
  84.0 6.6 %copy-start.5 = (bf16[1024,192]{0,1:T(8,128)(2,1)}, bf16[1024,192]{0,1:T(8,128)(2,1)S(1)}, u32[]{:S(2)}) copy-start(bf16[1024,192]{0,1:T(8,128)(2,1)S(1)} %constant_dynamic-update-slice_fusion.1) | copy-start | bytes 1179652
  90.8 5.4 %copy-start.9 = (f32[192]{0:T(256)S(1)}, f32[192]{0:T(256)}, u32[]{:S(2)}) copy-start(f32[192]{0:T(256)} %constant.188.clone) | copy-start | bytes 2308
  90.8 5.4 %copy-start.10 = (f32[192]{0:T(256)S(1)}, f32[192]{0:T(256)}, u32[]{:S(2)}) copy-start(f32[192]{0:T(256)} %constant.190.clone) | copy-start | bytes 2308
  90.8 5.4 %copy-start.11 = (f32[192]{0:T(256)S(1)}, f32[192]{0:T(256)}, u32[]{:S(2)}) copy-start(f32[192]{0:T(256)} %constant.192.clone) | copy-start | bytes 2308
  90.8 5.4 %copy-start.12 = (f32[192]{0:T(256)S(1)}, f32[192]{0:T(256)}, u32[]{:S(2)}) copy-start(f32[192]{0:T(256)} %constant.194.clone) | copy-start | bytes 2308
  92.0 31.4 %collective-permute-start.1 = (bf16[2,1024,192]{1,2,0:T(8,128)(2,1)}, bf16[2,1024,192]{1,2,0:T(8,128)(2,1)}, u32[]{:S(2)}, u32[]{:S(2)}) collective-permute-start(bf16[2,1024,192]{1,2,0:T(8,128)(2,1)} %copy.131), channel_id=1, source_target_pairs={{0,8},{4,12},{8,0},{12,4},{1,9},{5,13},{9,1},{13,5},{2,10},{6,14},... | collective-permute-start | bytes 2359304 | tf_op jit(solution)/shard_map/ppermute | solution.py:35
  124.8 27.2 %copy-start.7 = (f32[192]{0:T(256)S(1)}, f32[192]{0:T(256)}, u32[]{:S(2)}) copy-start(f32[192]{0:T(256)} %constant.184.clone) | copy-start | bytes 2308
  124.9 27.2 %copy-start.8 = (f32[192]{0:T(256)S(1)}, f32[192]{0:T(256)}, u32[]{:S(2)}) copy-start(f32[192]{0:T(256)} %constant.186.clone) | copy-start | bytes 2308
  152.0 1.8 %copy-start.13 = (pred[4]{0:T(512)(128)(4,1)S(1)}, pred[4]{0:T(512)(128)(4,1)}, u32[]{:S(2)}) copy-start(pred[4]{0:T(512)(128)(4,1)} %constant.185.clone) | copy-start | bytes 16
  152.0 1.8 %copy-start.14 = (pred[4]{0:T(512)(128)(4,1)S(1)}, pred[4]{0:T(512)(128)(4,1)}, u32[]{:S(2)}) copy-start(pred[4]{0:T(512)(128)(4,1)} %constant.187.clone) | copy-start | bytes 16
  152.2 2.3 %copy-start.6 = (f32[4,256,4]{1,2,0:T(4,128)S(1)}, f32[4,256,4]{1,2,0:T(4,128)}, u32[]{:S(2)}) copy-start(f32[4,256,4]{1,2,0:T(4,128)} %get-tuple-element.113) | copy-start | bytes 49156
  (3 other events, 5.3 us)
